TPU v7x, 256 devices: a whole 4x4x8 slice. The times are simulated.
256 devices in a mesh: depth: 8 (over y_lo, x), gx: 32 (over z, y_hi, core).
Axes of the slice: x: 4, y: 4 (y_hi: 2, y_lo: 2; y = y_hi * 2 + y_lo), z: 8, core: 2. Of those that a mesh axis runs over, the one named last changes fastest.
Arguments:
- offset_image: bfloat16 [64, 128, 128, 256], P(None, 'depth', 'gx'), may hold values from -6 to 6
- dip_class: int32 [128, 128, 256], P('depth', 'gx'), may hold values from 0 to 7
- slant_taper: bfloat16 [64, 64, 33], replicated, may hold values from -0.3125 to 0.3125
- band_offsets: int32 [64], replicated, may hold values from -14 to 14
- coefficients: float32 [8, 27], replicated, may hold values from -1.25 to 1.25
Outputs:
- smoothed: bfloat16 [64, 128, 128, 256], P(None, 'depth', 'gx')
All inputs are finite; a program needn't handle non-finite values.
Results may differ from a plain program's by a relative error of at most 0.0049.
Values may be sent and summed in bfloat16 or wider, within the bound.
No kernel may reach another device: no remote copies, remote signals or barrier semaphores. Data moves between devices by JAX's collectives and lax.ppermute only.
A program may use at most 64 MiB of HBM per device.

v0:
```python
import jax
import jax.numpy as jnp
from jax import lax
from jax.sharding import PartitionSpec as P

R = 16
BAND = 2
RX = 4
RY = 1


def with_halo(x, sides, width):
    for axis, dim in sides:
        count, length = (lax.axis_size(axis), x.shape[dim])
        up = [(i, (i + 1) % count) for i in range(count - 1)]
        down = [(j, i) for i, j in up]
        last = lax.slice_in_dim(x, length - width, length, axis=dim)
        leading = lax.slice_in_dim(x, 0, width, axis=dim)
        before = lax.ppermute(last, axis, up)
        after = lax.ppermute(leading, axis, down)
        x = jnp.concatenate([before, x, after], axis=dim)
    return x


def slant_matrix_of(slant_taper, band_offsets, offset_count):
    offset_index = jnp.arange(offset_count, dtype=jnp.int32)
    depth_shift = jnp.floor_divide(band_offsets[:, None] * offset_index[None, :], offset_count)
    reach_index = jnp.arange(slant_taper.shape[2], dtype=jnp.int32) - R
    inside_band = jnp.abs(reach_index[None, None, :] - depth_shift[:, :, None]) <= BAND
    return jnp.where(inside_band, slant_taper, jnp.zeros_like(slant_taper))


def slant_stack(slant_matrix, padded, depth_cells):

    def one_depth(depth_level):
        window = lax.dynamic_slice_in_dim(padded, depth_level, 2 * R + 1, 1)
        result = jnp.einsum(
            "ahd,hdxy->axy", slant_matrix, window, preferred_element_type=jnp.float32
        )
        return result.astype(jnp.bfloat16)

    return lax.map(one_depth, jnp.arange(depth_cells, dtype=jnp.int32))


def dip_weights(dip_class, coefficients):
    class_index = jnp.arange(coefficients.shape[0], dtype=jnp.int32)
    onehot = (dip_class[None] == class_index[:, None, None, None]).astype(jnp.float32)
    return jnp.einsum("qt,qzxy->tzxy", coefficients, onehot, precision=lax.Precision.HIGHEST)


def smooth_all(gathers, tap_weights, lateral_cells, cross_cells):
    padded_rows = jnp.pad(gathers, ((0, 0), (0, 0), (0, 0), (RY, RY)))
    running = jnp.zeros(
        (gathers.shape[0], gathers.shape[1], lateral_cells, cross_cells), jnp.float32
    )
    for column_step in range(2 * RX + 1):
        for row_step in range(2 * RY + 1):
            tap_index = column_step * (2 * RY + 1) + row_step
            shifted = padded_rows[
                :, :, column_step : column_step + lateral_cells, row_step : row_step + cross_cells
            ]
            running = running + tap_weights[tap_index][:, None] * shifted.astype(jnp.float32)
    return jnp.moveaxis(running.astype(jnp.bfloat16), 0, 1)


def depth_extend(offset_image):
    return with_halo(offset_image, (("depth", 1),), R)


def local(offset_image, dip_class, slant_taper, band_offsets, coefficients):
    offset_count, depth_cells, lateral_cells, cross_cells = offset_image.shape
    slant_matrix = slant_matrix_of(slant_taper, band_offsets, offset_count)
    padded = depth_extend(offset_image)
    local_gathers = slant_stack(slant_matrix, padded, depth_cells)
    gathers = with_halo(local_gathers, (("gx", 2),), RX)
    tap_weights = dip_weights(dip_class, coefficients)
    return smooth_all(gathers, tap_weights, lateral_cells, cross_cells)


def solution(mesh):
    return jax.shard_map(
        local,
        mesh=mesh,
        in_specs=(P(None, "depth", "gx", None), P("depth", "gx", None), P(), P(), P()),
        out_specs=P(None, "depth", "gx", None),
        check_vma=False,
    )
```

profile of v0, /device:TPU:137, one launch (start us, length us, event | category | flops | bytes accessed | tf_op | source)
XLA Modules:
  0.0 286.1 jit_solution(5365541204077641517)
XLA Ops:
  0.0 4.1 %copy.6 = bf16[64,16,4,256]{3,0,1,2:T(8,128)(2,1)} copy(bf16[64,16,4,256]{3,2,1,0:T(4,128)(2,1)} %param.7) | data formatting | bytes 4194304 | tf_op args[0]
  4.2 4.3 %collective-permute-start.1 = (bf16[64,16,4,256]{3,0,1,2:T(8,128)(2,1)}, bf16[64,16,4,256]{3,0,1,2:T(8,128)(2,1)}, u32[]{:S(2)}, u32[]{:S(2)}) collective-permute-start(bf16[64,16,4,256]{3,0,1,2:T(8,128)(2,1)} %copy.6), channel_id=1, source_target_pairs={{32,0},{64,32},{96,64},{128,96},{160,128},{192,160},{224,192},{33,... | collective-permute-start | bytes 6291464 | tf_op jit(solution)/shard_map/ppermute | solution.py:20
  8.4 1.9 collective-permute-start
  13.6 1.8 fusion.30
  15.5 37.6 %collective-permute-done.1 = bf16[64,16,4,256]{3,0,1,2:T(8,128)(2,1)} collective-permute-done((bf16[64,16,4,256]{3,0,1,2:T(8,128)(2,1)}, bf16[64,16,4,256]{3,0,1,2:T(8,128)(2,1)}, u32[]{:S(2)}, u32[]{:S(2)}) %collective-permute-start.1) | collective-permute-done | bytes 2097184 | tf_op jit(solution)/shard_map/ppermute | solution.py:20
  53.0 5.9 %collective-permute-done = bf16[64,16,4,256]{3,0,1,2:T(8,128)(2,1)} collective-permute-done((bf16[64,16,4,256]{3,0,1,2:T(8,128)(2,1)}, bf16[64,16,4,256]{3,0,1,2:T(8,128)(2,1)}, u32[]{:S(2)}, u32[]{:S(2)}) %collective-permute-start) | collective-permute-done | bytes 2097184 | tf_op jit(solution)/shard_map/ppermute | solution.py:19
  59.0 6.0 %pad_maximum_fusion = bf16[64,48,4,256]{3,0,1,2:T(8,128)(2,1)} fusion(bf16[64,16,4,256]{3,0,1,2:T(8,128)(2,1)} %collective-permute-done.1, bf16[64,16,4,256]{3,0,1,2:T(8,128)(2,1)} %copy.6, bf16[64,16,4,256]{3,0,1,2:T(8,128)(2,1)} %collective-permute-done), kind=kLoop, calls=%fused_computation.16 | loop fusion | flops 6291456 | bytes 12582912 | tf_op jit(solution)/shard_map/concatenate | solution.py:21
  65.0 93.4 %while.10 = (s32[]{:T(128)}, bf16[16,64,4,256]{3,2,0,1:T(4,128)(2,1)S(1)}, s32[16]{0:T(128)S(1)}, bf16[64,48,4,256]{3,0,1,2:T(8,128)(2,1)}, bf16[64,64,33]{1,0,2...) while((s32[]{:T(128)}, bf16[16,64,4,256]{3,2,0,1:T(4,128)(2,1)S(1)}, s32[16]{0:T(128)S(1)}, ...), condition=%wide.region_1.2_spmd, body=%wide.region_0.1_spmd.sunk | while | flops 276889600 | bytes 4989075 | solution.py:42
  67.5 3.1 %fusion.37 = bf16[1,64,4,256]{3,1,2,0:T(8,128)(2,1)S(1)} fusion(bf16[64,48,4,256]{3,0,1,2:T(8,128)(2,1)} %get-tuple-element.146, s32[]{:T(128)S(6)} %select_n.21, bf16[64,64,33]{1,0,2:T(8,128)(2,1)S(1)} %get-tuple-element.147), kind=kOutput, calls=%fused_computation.4.clone.1 | convolution fusion | flops 276889600 | bytes 4726788 | tf_op jit(solution)/shard_map/while/body/eval_jaxpr/ahd,hdxy->axy/dot_general | solution.py:37
  73.3 3.1 %fusion.37 = bf16[1,64,4,256]{3,1,2,0:T(8,128)(2,1)S(1)} fusion(bf16[64,48,4,256]{3,0,1,2:T(8,128)(2,1)} %get-tuple-element.146, s32[]{:T(128)S(6)} %select_n.21, bf16[64,64,33]{1,0,2:T(8,128)(2,1)S(1)} %get-tuple-element.147), kind=kOutput, calls=%fused_computation.4.clone.1 | convolution fusion | flops 276889600 | bytes 4726788 | tf_op jit(solution)/shard_map/while/body/eval_jaxpr/ahd,hdxy->axy/dot_general | solution.py:37
  79.2 3.1 %fusion.37 = bf16[1,64,4,256]{3,1,2,0:T(8,128)(2,1)S(1)} fusion(bf16[64,48,4,256]{3,0,1,2:T(8,128)(2,1)} %get-tuple-element.146, s32[]{:T(128)S(6)} %select_n.21, bf16[64,64,33]{1,0,2:T(8,128)(2,1)S(1)} %get-tuple-element.147), kind=kOutput, calls=%fused_computation.4.clone.1 | convolution fusion | flops 276889600 | bytes 4726788 | tf_op jit(solution)/shard_map/while/body/eval_jaxpr/ahd,hdxy->axy/dot_general | solution.py:37
  85.0 3.1 %fusion.37 = bf16[1,64,4,256]{3,1,2,0:T(8,128)(2,1)S(1)} fusion(bf16[64,48,4,256]{3,0,1,2:T(8,128)(2,1)} %get-tuple-element.146, s32[]{:T(128)S(6)} %select_n.21, bf16[64,64,33]{1,0,2:T(8,128)(2,1)S(1)} %get-tuple-element.147), kind=kOutput, calls=%fused_computation.4.clone.1 | convolution fusion | flops 276889600 | bytes 4726788 | tf_op jit(solution)/shard_map/while/body/eval_jaxpr/ahd,hdxy->axy/dot_general | solution.py:37
  90.9 3.1 %fusion.37 = bf16[1,64,4,256]{3,1,2,0:T(8,128)(2,1)S(1)} fusion(bf16[64,48,4,256]{3,0,1,2:T(8,128)(2,1)} %get-tuple-element.146, s32[]{:T(128)S(6)} %select_n.21, bf16[64,64,33]{1,0,2:T(8,128)(2,1)S(1)} %get-tuple-element.147), kind=kOutput, calls=%fused_computation.4.clone.1 | convolution fusion | flops 276889600 | bytes 4726788 | tf_op jit(solution)/shard_map/while/body/eval_jaxpr/ahd,hdxy->axy/dot_general | solution.py:37
  96.7 3.1 %fusion.37 = bf16[1,64,4,256]{3,1,2,0:T(8,128)(2,1)S(1)} fusion(bf16[64,48,4,256]{3,0,1,2:T(8,128)(2,1)} %get-tuple-element.146, s32[]{:T(128)S(6)} %select_n.21, bf16[64,64,33]{1,0,2:T(8,128)(2,1)S(1)} %get-tuple-element.147), kind=kOutput, calls=%fused_computation.4.clone.1 | convolution fusion | flops 276889600 | bytes 4726788 | tf_op jit(solution)/shard_map/while/body/eval_jaxpr/ahd,hdxy->axy/dot_general | solution.py:37
  102.5 3.1 %fusion.37 = bf16[1,64,4,256]{3,1,2,0:T(8,128)(2,1)S(1)} fusion(bf16[64,48,4,256]{3,0,1,2:T(8,128)(2,1)} %get-tuple-element.146, s32[]{:T(128)S(6)} %select_n.21, bf16[64,64,33]{1,0,2:T(8,128)(2,1)S(1)} %get-tuple-element.147), kind=kOutput, calls=%fused_computation.4.clone.1 | convolution fusion | flops 276889600 | bytes 4726788 | tf_op jit(solution)/shard_map/while/body/eval_jaxpr/ahd,hdxy->axy/dot_general | solution.py:37
  108.4 3.1 %fusion.37 = bf16[1,64,4,256]{3,1,2,0:T(8,128)(2,1)S(1)} fusion(bf16[64,48,4,256]{3,0,1,2:T(8,128)(2,1)} %get-tuple-element.146, s32[]{:T(128)S(6)} %select_n.21, bf16[64,64,33]{1,0,2:T(8,128)(2,1)S(1)} %get-tuple-element.147), kind=kOutput, calls=%fused_computation.4.clone.1 | convolution fusion | flops 276889600 | bytes 4726788 | tf_op jit(solution)/shard_map/while/body/eval_jaxpr/ahd,hdxy->axy/dot_general | solution.py:37
  114.2 3.1 %fusion.37 = bf16[1,64,4,256]{3,1,2,0:T(8,128)(2,1)S(1)} fusion(bf16[64,48,4,256]{3,0,1,2:T(8,128)(2,1)} %get-tuple-element.146, s32[]{:T(128)S(6)} %select_n.21, bf16[64,64,33]{1,0,2:T(8,128)(2,1)S(1)} %get-tuple-element.147), kind=kOutput, calls=%fused_computation.4.clone.1 | convolution fusion | flops 276889600 | bytes 4726788 | tf_op jit(solution)/shard_map/while/body/eval_jaxpr/ahd,hdxy->axy/dot_general | solution.py:37
  120.1 3.1 %fusion.37 = bf16[1,64,4,256]{3,1,2,0:T(8,128)(2,1)S(1)} fusion(bf16[64,48,4,256]{3,0,1,2:T(8,128)(2,1)} %get-tuple-element.146, s32[]{:T(128)S(6)} %select_n.21, bf16[64,64,33]{1,0,2:T(8,128)(2,1)S(1)} %get-tuple-element.147), kind=kOutput, calls=%fused_computation.4.clone.1 | convolution fusion | flops 276889600 | bytes 4726788 | tf_op jit(solution)/shard_map/while/body/eval_jaxpr/ahd,hdxy->axy/dot_general | solution.py:37
  125.9 3.1 %fusion.37 = bf16[1,64,4,256]{3,1,2,0:T(8,128)(2,1)S(1)} fusion(bf16[64,48,4,256]{3,0,1,2:T(8,128)(2,1)} %get-tuple-element.146, s32[]{:T(128)S(6)} %select_n.21, bf16[64,64,33]{1,0,2:T(8,128)(2,1)S(1)} %get-tuple-element.147), kind=kOutput, calls=%fused_computation.4.clone.1 | convolution fusion | flops 276889600 | bytes 4726788 | tf_op jit(solution)/shard_map/while/body/eval_jaxpr/ahd,hdxy->axy/dot_general | solution.py:37
  131.7 3.1 %fusion.37 = bf16[1,64,4,256]{3,1,2,0:T(8,128)(2,1)S(1)} fusion(bf16[64,48,4,256]{3,0,1,2:T(8,128)(2,1)} %get-tuple-element.146, s32[]{:T(128)S(6)} %select_n.21, bf16[64,64,33]{1,0,2:T(8,128)(2,1)S(1)} %get-tuple-element.147), kind=kOutput, calls=%fused_computation.4.clone.1 | convolution fusion | flops 276889600 | bytes 4726788 | tf_op jit(solution)/shard_map/while/body/eval_jaxpr/ahd,hdxy->axy/dot_general | solution.py:37
  137.6 3.1 %fusion.37 = bf16[1,64,4,256]{3,1,2,0:T(8,128)(2,1)S(1)} fusion(bf16[64,48,4,256]{3,0,1,2:T(8,128)(2,1)} %get-tuple-element.146, s32[]{:T(128)S(6)} %select_n.21, bf16[64,64,33]{1,0,2:T(8,128)(2,1)S(1)} %get-tuple-element.147), kind=kOutput, calls=%fused_computation.4.clone.1 | convolution fusion | flops 276889600 | bytes 4726788 | tf_op jit(solution)/shard_map/while/body/eval_jaxpr/ahd,hdxy->axy/dot_general | solution.py:37
  143.4 3.1 %fusion.37 = bf16[1,64,4,256]{3,1,2,0:T(8,128)(2,1)S(1)} fusion(bf16[64,48,4,256]{3,0,1,2:T(8,128)(2,1)} %get-tuple-element.146, s32[]{:T(128)S(6)} %select_n.21, bf16[64,64,33]{1,0,2:T(8,128)(2,1)S(1)} %get-tuple-element.147), kind=kOutput, calls=%fused_computation.4.clone.1 | convolution fusion | flops 276889600 | bytes 4726788 | tf_op jit(solution)/shard_map/while/body/eval_jaxpr/ahd,hdxy->axy/dot_general | solution.py:37
  149.3 3.1 %fusion.37 = bf16[1,64,4,256]{3,1,2,0:T(8,128)(2,1)S(1)} fusion(bf16[64,48,4,256]{3,0,1,2:T(8,128)(2,1)} %get-tuple-element.146, s32[]{:T(128)S(6)} %select_n.21, bf16[64,64,33]{1,0,2:T(8,128)(2,1)S(1)} %get-tuple-element.147), kind=kOutput, calls=%fused_computation.4.clone.1 | convolution fusion | flops 276889600 | bytes 4726788 | tf_op jit(solution)/shard_map/while/body/eval_jaxpr/ahd,hdxy->axy/dot_general | solution.py:37
  155.1 3.1 %fusion.37 = bf16[1,64,4,256]{3,1,2,0:T(8,128)(2,1)S(1)} fusion(bf16[64,48,4,256]{3,0,1,2:T(8,128)(2,1)} %get-tuple-element.146, s32[]{:T(128)S(6)} %select_n.21, bf16[64,64,33]{1,0,2:T(8,128)(2,1)S(1)} %get-tuple-element.147), kind=kOutput, calls=%fused_computation.4.clone.1 | convolution fusion | flops 276889600 | bytes 4726788 | tf_op jit(solution)/shard_map/while/body/eval_jaxpr/ahd,hdxy->axy/dot_general | solution.py:37
  158.4 5.9 %collective-permute-start.2 = (bf16[16,64,4,256]{3,2,0,1:T(4,128)(2,1)S(1)}, bf16[16,64,4,256]{3,2,0,1:T(4,128)(2,1)S(1)}, u32[]{:S(2)}, u32[]{:S(2)}) collective-permute-start(bf16[16,64,4,256]{3,2,0,1:T(4,128)(2,1)S(1)} %get-tuple-element.32), channel_id=1, source_target_pairs={{0,1},{1,2},{2,3},{3,4},{4,5},{5,6},{6,7},{7,8},{8,9},{9,10},{10,1... | collective-permute-start | bytes 6291464 | tf_op jit(solution)/shard_map/ppermute | solution.py:19
  164.3 2.1 collective-permute-start.3
  169.0 1.6 copy_bitcast_fusion.6
  172.2 1.6 copy_bitcast_fusion.10
  178.4 31.4 %collective-permute-done.2 = bf16[16,64,4,256]{3,2,0,1:T(4,128)(2,1)S(1)} collective-permute-done((bf16[16,64,4,256]{3,2,0,1:T(4,128)(2,1)S(1)}, bf16[16,64,4,256]{3,2,0,1:T(4,128)(2,1)S(1)}, u32[]{:S(2)}, u32[]{:S(2)}) %collective-permute-start.2) | collective-permute-done | bytes 2097184 | tf_op jit(solution)/shard_map/ppermute | solution.py:19
  209.8 3.2 %collective-permute-done.3 = bf16[16,64,4,256]{3,2,0,1:T(4,128)(2,1)S(1)} collective-permute-done((bf16[16,64,4,256]{3,2,0,1:T(4,128)(2,1)S(1)}, bf16[16,64,4,256]{3,2,0,1:T(4,128)(2,1)S(1)}, u32[]{:S(2)}, u32[]{:S(2)}) %collective-permute-start.3) | collective-permute-done | bytes 2097184 | tf_op jit(solution)/shard_map/ppermute | solution.py:20
  213.0 16.2 %fusion.18 = bf16[16,64,12,258]{3,2,0,1:T(8,128)(2,1)S(1)} fusion(bf16[16,64,4,256]{3,2,0,1:T(4,128)(2,1)S(1)} %collective-permute-done.3, bf16[16,64,4,256]{3,2,0,1:T(4,128)(2,1)} %copy-done.3, bf16[16,64,4,256]{3,2,0,1:T(4,128)(2,1)S(1)} %collective-permute-done.2), kind=kLoop, calls=%fused_computation.15 | loop fusion | flops 38043648 | bytes 12632064 | tf_op jit(solution)/shard_map/concatenate | solution.py:21
  229.2 56.7 %fusion.23 = bf16[64,16,4,256]{3,2,1,0:T(4,128)(2,1)} fusion(bf16[16,64,12,258]{3,2,0,1:T(8,128)(2,1)S(1)} %fusion.18, f32[16,4,256]{2,1,0:T(4,128)S(1)} %get-tuple-element.70, bf16[16,64,4,256]{3,2,0,1:T(4,128)(2,1)} %copy-done.2, f32[16,4,256]{2,1,0:T(4,128)S(1)} %get-tuple-element.71, f32[16,4,256]{2,1,0:T(4,128)S(1)} %get-tuple-element.72, ...), kind=kLoop, calls=%fused_computation.32 | loop fusion | flops 103809024 | bytes 47906816 | tf_op jit(solution)/shard_map/transpose | solution.py:63
  (75 shorter events, 23.5 us)
Async XLA Ops:
  0.0 10.5 %copy-start = (f32[8,27]{1,0:T(8,128)S(1)}, f32[8,27]{1,0:T(8,128)}, u32[]{:S(2)}) copy-start(f32[8,27]{1,0:T(8,128)} %param.11) | copy-start | bytes 2596
  0.0 10.4 %copy-start.11 = (s32[64]{0:T(128)S(1)}, s32[64]{0:T(128)}, u32[]{:S(2)}) copy-start(s32[64]{0:T(128)} %param.10) | copy-start | bytes 772
  0.0 10.5 %copy-start.10 = (s32[16,4,256]{2,1,0:T(4,128)S(1)}, s32[16,4,256]{2,1,0:T(4,128)}, u32[]{:S(2)}) copy-start(s32[16,4,256]{2,1,0:T(4,128)} %param.8) | copy-start | bytes 196612
  0.0 13.3 %copy-start.4 = (bf16[64,64,33]{1,0,2:T(8,128)(2,1)S(1)}, bf16[64,64,33]{1,0,2:T(8,128)(2,1)}, u32[]{:S(2)}) copy-start(bf16[64,64,33]{1,0,2:T(8,128)(2,1)} %param.9) | copy-start | bytes 811012
  4.2 48.9 %collective-permute-start.1 = (bf16[64,16,4,256]{3,0,1,2:T(8,128)(2,1)}, bf16[64,16,4,256]{3,0,1,2:T(8,128)(2,1)}, u32[]{:S(2)}, u32[]{:S(2)}) collective-permute-start(bf16[64,16,4,256]{3,0,1,2:T(8,128)(2,1)} %copy.6), channel_id=1, source_target_pairs={{32,0},{64,32},{96,64},{128,96},{160,128},{192,160},{224,192},{33,... | collective-permute-start | bytes 6291464 | tf_op jit(solution)/shard_map/ppermute | solution.py:20
  8.4 50.6 %collective-permute-start = (bf16[64,16,4,256]{3,0,1,2:T(8,128)(2,1)}, bf16[64,16,4,256]{3,0,1,2:T(8,128)(2,1)}, u32[]{:S(2)}, u32[]{:S(2)}) collective-permute-start(bf16[64,16,4,256]{3,0,1,2:T(8,128)(2,1)} %copy.6), channel_id=1, source_target_pairs={{0,32},{32,64},{64,96},{96,128},{128,160},{160,192},{192,224},{1,3... | collective-permute-start | bytes 6291464 | tf_op jit(solution)/shard_map/ppermute | solution.py:19
  65.0 101.5 %copy-start.8 = (f32[1,16,4,256]{3,0,2,1:T(1,128)S(1)}, f32[1,16,4,256]{3,0,2,1:T(1,128)}, u32[]{:S(2)}) copy-start(f32[1,16,4,256]{3,0,2,1:T(1,128)} %get-tuple-element.67) | copy-start | bytes 196612
  65.0 101.5 %copy-start.9 = (f32[1,16,4,256]{3,0,2,1:T(1,128)S(1)}, f32[1,16,4,256]{3,0,2,1:T(1,128)}, u32[]{:S(2)}) copy-start(f32[1,16,4,256]{3,0,2,1:T(1,128)} %get-tuple-element.68) | copy-start | bytes 196612
  158.4 51.4 %copy-start.3 = (bf16[16,64,4,256]{3,2,0,1:T(4,128)(2,1)}, bf16[16,64,4,256]{3,2,0,1:T(4,128)(2,1)S(1)}, u32[]{:S(2)}) copy-start(bf16[16,64,4,256]{3,2,0,1:T(4,128)(2,1)S(1)} %get-tuple-element.32) | copy-start | bytes 6291460
  158.4 51.4 %collective-permute-start.2 = (bf16[16,64,4,256]{3,2,0,1:T(4,128)(2,1)S(1)}, bf16[16,64,4,256]{3,2,0,1:T(4,128)(2,1)S(1)}, u32[]{:S(2)}, u32[]{:S(2)}) collective-permute-start(bf16[16,64,4,256]{3,2,0,1:T(4,128)(2,1)S(1)} %get-tuple-element.32), channel_id=1, source_target_pairs={{0,1},{1,2},{2,3},{3,4},{4,5},{5,6},{6,7},{7,8},{8,9},{9,10},{10,1... | collective-permute-start | bytes 6291464 | tf_op jit(solution)/shard_map/ppermute | solution.py:19
  164.3 48.6 %collective-permute-start.3 = (bf16[16,64,4,256]{3,2,0,1:T(4,128)(2,1)S(1)}, bf16[16,64,4,256]{3,2,0,1:T(4,128)(2,1)S(1)}, u32[]{:S(2)}, u32[]{:S(2)}) collective-permute-start(bf16[16,64,4,256]{3,2,0,1:T(4,128)(2,1)S(1)} %get-tuple-element.32), channel_id=1, source_target_pairs={{1,0},{2,1},{3,2},{4,3},{5,4},{6,5},{7,6},{8,7},{9,8},{10,9},{11,1... | collective-permute-start | bytes 6291464 | tf_op jit(solution)/shard_map/ppermute | solution.py:20
  178.4 50.8 %copy-start.5 = (f32[16,4,256]{2,1,0:T(4,128)S(1)}, f32[16,4,256]{2,1,0:T(4,128)}, u32[]{:S(2)}) copy-start(f32[16,4,256]{2,1,0:T(4,128)} %get-tuple-element.91) | copy-start | bytes 196612
  209.8 19.4 %copy-start.1 = (bf16[16,64,4,256]{3,2,0,1:T(4,128)(2,1)}, bf16[16,64,4,256]{3,2,0,1:T(4,128)(2,1)S(1)}, u32[]{:S(2)}) copy-start(bf16[16,64,4,256]{3,2,0,1:T(4,128)(2,1)S(1)} %collective-permute-done.2) | copy-start | bytes 6291460
  213.0 16.2 %copy-start.2 = (bf16[16,64,4,256]{3,2,0,1:T(4,128)(2,1)}, bf16[16,64,4,256]{3,2,0,1:T(4,128)(2,1)S(1)}, u32[]{:S(2)}) copy-start(bf16[16,64,4,256]{3,2,0,1:T(4,128)(2,1)S(1)} %collective-permute-done.3) | copy-start | bytes 6291460
  213.0 16.2 %copy-start.6 = (f32[16,4,256]{2,1,0:T(4,128)S(1)}, f32[16,4,256]{2,1,0:T(4,128)}, u32[]{:S(2)}) copy-start(f32[16,4,256]{2,1,0:T(4,128)} %get-tuple-element.86) | copy-start | bytes 196612
  213.0 16.2 %copy-start.7 = (f32[16,4,256]{2,1,0:T(4,128)S(1)}, f32[16,4,256]{2,1,0:T(4,128)}, u32[]{:S(2)}) copy-start(f32[16,4,256]{2,1,0:T(4,128)} %get-tuple-element.87) | copy-start | bytes 196612
where the time goes:
time: 288 us; the launch traced here: 286 us
  other arithmetic  79.3 us (28%)
  waiting for transfers between devices  78.1 us (27%)
  matrix products  51.4 us (18%)
  loops' own time  31.6 us (11%)
  local copies, waits for them, and re-layouts  31.1 us (11%)
  starting transfers between devices  14.2 us (5%)
    transpose x1, other arithmetic, smooth_all(): return jnp.moveaxis(running.astype(jnp.bfloat16), 0, 1)  56.7 us
    dot_general x16, matrix products, one_depth(): jnp.einsum('ahd,hdxy->axy', slant_matrix, window, preferred_element_type=...  50.4 us
    ppermute x2, waiting for transfers between devices, with_halo(): after = lax.ppermute(leading, axis, down)  40.8 us
    ppermute x2, waiting for transfers between devices, with_halo(): before = lax.ppermute(last, axis, up)  37.4 us
    another operation x1, loops' own time, slant_stack(): return lax.map(one_depth, jnp.arange(depth_cells, dtype=jnp.int32))  31.6 us
    concatenate x2, other arithmetic, with_halo(): x = jnp.concatenate([before, x, after], axis=dim)  22.1 us
    unnamed x39, local copies, waits for them, and re-layouts  16.8 us
    dynamic_slice x16, local copies, waits for them, and re-layouts, slant_stack(): return lax.map(one_depth, jnp.arange(depth_cells, dtype=jnp.int32))  9.38 us
  transfers between devices with their start and end apart: 4, of which 4 were waited for; matrix products, arithmetic and copies ran while one was open for 6% of the time, Pallas kernels for 0%

commit v1 on v0

v1 whole, which is shorter than its diff:
```python
import functools

import jax
import jax.numpy as jnp
from jax import lax
from jax.experimental import pallas as pl
from jax.experimental.pallas import tpu as pltpu
from jax.sharding import PartitionSpec as P

R = 16
BAND = 2
RX = 4
RY = 1
REACH = R - BAND
ZB = 4
BF = jnp.bfloat16
F32 = jnp.float32


def reach_tables(offsets, steps):
    before, after = [], []
    for k in range(1, steps + 1):
        low = [h for h in range(offsets) if -((-REACH * h) // offsets) + BAND >= k]
        high = [h for h in range(offsets) if (REACH * h) // offsets + BAND >= k]
        if low:
            before.append(low[0])
        if high:
            after.append(high[0])
    return before, after


def segments(firsts, offsets):
    out, at = [], 0
    for first in firsts:
        out.append((at, offsets - first))
        at += offsets - first
    return out, at


def spec():
    return pl.BlockSpec(memory_space=pltpu.VMEM)


def cost(flops, moved):
    return pl.CostEstimate(flops=flops, bytes_accessed=moved, transcendentals=0)


def swap_matrix(offsets, columns):
    n = offsets * columns
    row = lax.broadcasted_iota(jnp.int32, (n, n), 0)
    col = lax.broadcasted_iota(jnp.int32, (n, n), 1)
    hit = col == (row % offsets) * columns + row // offsets
    return jnp.where(hit, 1.0, 0.0).astype(BF)


def to_columns(swap, planes):
    h, x, y = planes.shape
    moved = jnp.dot(swap, planes.reshape(h * x, y), preferred_element_type=F32)
    return moved.astype(BF).reshape(x, h, y)


def pack_kernel(before, after, image, up, down):
    h, z = image.shape[:2]
    for k, (at, n) in enumerate(segments(before, h)[0]):
        up[at : at + n] = image[h - n : h, z - 1 - k]
    for k, (at, n) in enumerate(segments(after, h)[0]):
        down[at : at + n] = image[h - n : h, k]


def pack(image, before, after):
    h, z, x, y = image.shape
    n_up, n_down = segments(before, h)[1], segments(after, h)[1]
    return pl.pallas_call(
        functools.partial(pack_kernel, before, after),
        out_shape=(
            jax.ShapeDtypeStruct((n_up, x, y), BF),
            jax.ShapeDtypeStruct((n_down, x, y), BF),
        ),
        in_specs=[spec()],
        out_specs=(spec(), spec()),
        name="pack",
    )(image)


def local_kernel(image, coefficients, dip, columns, weights):
    h, z, x, y = image.shape
    swap = swap_matrix(h, x)
    for level in range(z):
        columns[:, level * h : (level + 1) * h, :] = to_columns(swap, image[:, level])
    lane = lax.broadcasted_iota(jnp.int32, (z * x, y), 1)
    classes = dip[...]
    tests = [classes == q for q in range(1, coefficients.shape[0])]
    for t in range(weights.shape[0]):
        w = jnp.full((z * x, y), coefficients[0, t], F32)
        for q, test in enumerate(tests):
            w = jnp.where(test, coefficients[q + 1, t], w)
        shift = t % (2 * RY + 1) - RY
        if shift:
            w = pltpu.roll(w, shift % y, 1)
            w = jnp.where(lane < shift if shift > 0 else lane >= y + shift, 0.0, w)
        weights[t] = w


def prepare(image, coefficients, dip):
    h, z, x, y = image.shape
    taps = coefficients.shape[1]
    return pl.pallas_call(
        local_kernel,
        out_shape=(
            jax.ShapeDtypeStruct((x, z * h, y), BF),
            jax.ShapeDtypeStruct((taps, z * x, y), F32),
        ),
        in_specs=[spec(), pl.BlockSpec(memory_space=pltpu.SMEM), spec()],
        out_specs=(spec(), spec()),
        cost_estimate=cost(2 * h * x * h * x * y * z, 8 << 20),
        name="prepare",
    )(image, coefficients, dip.reshape(z * x, y))


def stack_block(slant, low, mid, high, zb, x, tile):
    n_low = low.shape[1] - zb * tile
    n_mid = mid.shape[1]
    n_high = (zb + 1) * tile
    total = jnp.dot(slant[:, :n_low], low[x, zb * tile :, :], preferred_element_type=F32)
    total += jnp.dot(slant[:, n_low : n_low + n_mid], mid[x], preferred_element_type=F32)
    total += jnp.dot(slant[:, n_low + n_mid :], high[x, :n_high, :], preferred_element_type=F32)
    return total.astype(BF)


def first_kernel(before, after, slant, up, down, mid, gathers, low, high):
    h = slant.shape[1] // (2 * R + ZB)
    x = mid.shape[0]
    swap = swap_matrix(h, x)
    for k, (at, n) in enumerate(segments(before, h)[0]):
        plane = to_columns(swap, up[at + n - h : at + n])
        low[:, (R - 1 - k) * h : (R - k) * h, :] = plane
    for k, (at, n) in enumerate(segments(after, h)[0]):
        high[:, k * h : (k + 1) * h, :] = to_columns(swap, down[at + n - h : at + n])
    for k in range(len(after), R):
        high[:, k * h : (k + 1) * h, :] = jnp.zeros((x, h, high.shape[2]), BF)
    for column in range(x):
        gathers[column] = stack_block(slant, low, mid, high, 0, column, ZB * h)


def first_gathers(slant, up, down, mid, before, after):
    x, rows, y = mid.shape
    m = slant.shape[0]
    return pl.pallas_call(
        functools.partial(first_kernel, before, after),
        out_shape=(
            jax.ShapeDtypeStruct((x, m, y), BF),
            jax.ShapeDtypeStruct((x, rows, y), BF),
            jax.ShapeDtypeStruct((x, rows, y), BF),
        ),
        in_specs=[spec()] * 4,
        out_specs=(spec(),) * 3,
        cost_estimate=cost(2 * m * slant.shape[1] * x * y, 10 << 20),
        name="first",
    )(slant, up, down, mid)


def rest_kernel(slant, low, mid, high, *outs):
    h = slant.shape[1] // (2 * R + ZB)
    for n, out in enumerate(outs):
        for column in range(mid.shape[0]):
            out[column] = stack_block(slant, low, mid, high, n + 1, column, ZB * h)


def rest_gathers(slant, low, mid, high, count):
    x, rows, y = mid.shape
    m = slant.shape[0]
    return pl.pallas_call(
        rest_kernel,
        out_shape=(jax.ShapeDtypeStruct((x, m, y), BF),) * count,
        in_specs=[spec()] * 4,
        out_specs=(spec(),) * count,
        cost_estimate=cost(2 * count * m * slant.shape[1] * x * y, 9 << 20),
        name="rest",
    )(slant, low, mid, high)


def smooth_kernel(angles, weights, previous, own, following, *rest):
    out, scratch = rest[-2:]
    x, _, y = own.shape
    sources = (previous, own, following)
    n = angles * x
    row = lax.broadcasted_iota(jnp.int32, (n, n), 0)
    col = lax.broadcasted_iota(jnp.int32, (n, n), 1)
    swap = jnp.where(row == (col % angles) * x + col // angles, 1.0, 0.0).astype(BF)
    part = 32

    def level(j, carry):
        for column in range(x):
            for piece in range(angles // part):
                sums = [jnp.zeros((part, y), F32) for _ in range(2 * RY + 1)]
                for step in range(2 * RX + 1):
                    source = column + step - RX + x
                    rows = pl.ds(pl.multiple_of(j * angles + piece * part, part), part)
                    values = sources[source // x][source % x, rows, :].astype(F32)
                    for side in range(2 * RY + 1):
                        w = weights[step * (2 * RY + 1) + side, pl.ds(j * x + column, 1), :]
                        sums[side] = sums[side] + w * values
                total = sums[RY]
                for side in range(2 * RY + 1):
                    if side != RY:
                        total = total + pltpu.roll(sums[side], (RY - side) % y, 1)
                at = column * angles + piece * part
                scratch[at : at + part, :] = total.astype(BF)
        moved = jnp.dot(swap, scratch[...], preferred_element_type=F32)
        out[:, j] = moved.astype(BF).reshape(angles, x, y)
        return carry

    lax.fori_loop(0, ZB, level, 0)


def smooth(weights, previous, own, following, done, block, shape):
    angles, z, x, y = shape
    taps = weights.shape[0]
    whole = pl.BlockSpec(own.shape, lambda i: (0, 0, 0))
    in_specs = [pl.BlockSpec((taps, ZB * x, y), lambda i: (0, block, 0)), whole, whole, whole]
    operands = [weights, previous, own, following]
    aliases = {}
    if done is not None:
        in_specs.append(pl.BlockSpec(memory_space=pl.ANY))
        operands.append(done)
        aliases = {4: 0}
    return pl.pallas_call(
        functools.partial(smooth_kernel, angles),
        grid=(1,),
        out_shape=jax.ShapeDtypeStruct(shape, BF),
        in_specs=in_specs,
        out_specs=pl.BlockSpec((angles, ZB, x, y), lambda i: (0, block, 0, 0)),
        scratch_shapes=[pltpu.VMEM((angles * x, y), BF)],
        input_output_aliases=aliases,
        cost_estimate=cost(2 * taps * angles * ZB * x * y, 3 << 20),
        name="smooth",
    )(*operands)


def slant_matrix_of(slant_taper, band_offsets, offset_count):
    offset_index = jnp.arange(offset_count, dtype=jnp.int32)
    depth_shift = jnp.floor_divide(band_offsets[:, None] * offset_index[None, :], offset_count)
    reach_index = jnp.arange(slant_taper.shape[2], dtype=jnp.int32) - R
    inside_band = jnp.abs(reach_index[None, None, :] - depth_shift[:, :, None]) <= BAND
    return jnp.where(inside_band, slant_taper, jnp.zeros_like(slant_taper))


def block_matrix(slant_taper, band_offsets, offset_count):
    slant = slant_matrix_of(slant_taper, band_offsets, offset_count)
    angles, h, steps = slant.shape
    flat = jnp.transpose(slant, (0, 2, 1)).reshape(angles, steps * h)
    rows = [jnp.pad(flat, ((0, 0), (j * h, (ZB - 1 - j) * h))) for j in range(ZB)]
    return jnp.concatenate(rows, axis=0)


def exchange(x_up, x_down, axis):
    count = lax.axis_size(axis)
    up = [(i, i + 1) for i in range(count - 1)]
    down = [(j, i) for i, j in up]
    return lax.ppermute(x_up, axis, up), lax.ppermute(x_down, axis, down)


def local(offset_image, dip_class, slant_taper, band_offsets, coefficients):
    h, z, x, y = offset_image.shape
    angles = slant_taper.shape[0]
    before, after = reach_tables(h, R)
    up, down = pack(offset_image, before, after)
    up, down = exchange(up, down, "depth")
    mid, weights = prepare(offset_image, coefficients, dip_class)
    slant = block_matrix(slant_taper, band_offsets, h)
    first, low, high = first_gathers(slant, up, down, mid, before, after)
    blocks = z // ZB
    others = rest_gathers(slant, low, mid, high, blocks - 1)
    done = None
    for block, own in enumerate((first, *others)):
        previous, following = exchange(own, own, "gx")
        done = smooth(weights, previous, own, following, done, block, (angles, z, x, y))
    return done


def solution(mesh):
    return jax.shard_map(
        local,
        mesh=mesh,
        in_specs=(P(None, "depth", "gx", None), P("depth", "gx", None), P(), P(), P()),
        out_specs=P(None, "depth", "gx", None),
        check_vma=False,
    )
```

time: 288 us -> 127 us (0.44)
  the two profiles are of different devices: /device:TPU:137 before, /device:TPU:39 now
where the time goes in v1:
time: 127 us
  Pallas kernels  43.9 us (35%)
  waiting for transfers between devices  39.7 us (31%)
  starting transfers between devices  32.9 us (26%)
  local copies, waits for them, and re-layouts  8.41 us (7%)
  other arithmetic  1.78 us (1%)
    ppermute x10, waiting for transfers between devices, exchange(): return (lax.ppermute(x_up, axis, up), lax.ppermute(x_down, axis, down))  39.7 us
    ppermute x10, starting transfers between devices, exchange(): return (lax.ppermute(x_up, axis, up), lax.ppermute(x_down, axis, down))  32.9 us
    pallas_call x4, Pallas kernels, smooth(): pl.pallas_call(functools.partial(smooth_kernel, angles), grid=(1,), out_s...  21.2 us
    pallas_call x1, Pallas kernels, rest_gathers(): pl.pallas_call(rest_kernel, out_shape=(jax.ShapeDtypeStruct((x, m, y), BF...  7.88 us
    unnamed x28, local copies, waits for them, and re-layouts  7.06 us
    pallas_call x1, Pallas kernels, first_gathers(): pl.pallas_call(functools.partial(first_kernel, before, after), out_shape=...  6.41 us
    pallas_call x1, Pallas kernels, prepare(): pl.pallas_call(local_kernel, out_shape=(jax.ShapeDtypeStruct((x, z * h, y...  4.91 us
    pallas_call x1, Pallas kernels, pack(): pl.pallas_call(functools.partial(pack_kernel, before, after), out_shape=(...  3.47 us
  transfers between devices with their start and end apart: 10, of which 2 were waited for; matrix products, arithmetic and copies ran while one was open for 2% of the time, Pallas kernels for 16%

profile of v1, /device:TPU:39, one launch (start us, length us, event | category | flops | bytes accessed | tf_op | source)
XLA Modules:
  0.0 127.0 jit_solution(16472885506619938516)
XLA Ops:
  0.0 3.5 %pack.1 = (bf16[600,4,256]{2,1,0:T(4,128)(2,1)}, bf16[538,4,256]{2,1,0:T(4,128)(2,1)}) custom-call(bf16[64,16,4,256]{3,2,1,0:T(4,128)(2,1)} %image.3), custom_call_target="tpu_custom_call" | custom-call | tf_op jit(solution)/shard_map/pack/pallas_call | solution.py:73
  3.5 3.1 %collective-permute-start = (bf16[600,4,256]{2,1,0:T(4,128)(2,1)}, bf16[600,4,256]{2,1,0:T(4,128)(2,1)S(1)}, u32[]{:S(2)}, u32[]{:S(2)}) collective-permute-start(bf16[600,4,256]{2,1,0:T(4,128)(2,1)} %get-tuple-element.16), channel_id=1, source_target_pairs={{0,32},{32,64},{64,96},{96,128},{128,160},{160,192},{192,224},{1,3... | collective-permute-start | bytes 3686408 | tf_op jit(solution)/shard_map/ppermute | solution.py:260
  6.6 2.2 %collective-permute-start.1 = (bf16[538,4,256]{2,1,0:T(4,128)(2,1)}, bf16[538,4,256]{2,1,0:T(4,128)(2,1)S(1)}, u32[]{:S(2)}, u32[]{:S(2)}) collective-permute-start(bf16[538,4,256]{2,1,0:T(4,128)(2,1)} %get-tuple-element.17), channel_id=1, source_target_pairs={{32,0},{64,32},{96,64},{128,96},{160,128},{192,160},{224,192},{33,... | collective-permute-start | bytes 3305480 | tf_op jit(solution)/shard_map/ppermute | solution.py:260
  8.8 0.6 reshape.46.dip
  9.9 0.4 copy.10
  10.6 4.9 %prepare.1 = (bf16[4,1024,256]{2,1,0:T(8,128)(2,1)}, f32[27,64,256]{2,1,0:T(8,128)}) custom-call(bf16[64,16,4,256]{3,2,1,0:T(4,128)(2,1)} %image.3, f32[8,27]{1,0:T(8,128)} %coefficients.1, s32[64,256]{1,0:T(8,128)} %reshape.46.dip), custom_call_target="tpu_custom_call" | custom-call | flops 536870912 | bytes 8388608 | tf_op jit(solution)/shard_map/prepare/pallas_call | solution.py:107
  15.5 1.3 %fusion.7.slant = bf16[256,2304]{1,0:T(8,128)(2,1)} fusion(bf16[64,2112]{1,0:T(8,128)(2,1)S(1)} %reshape.47), kind=kLoop, calls=%fused_computation.13 | loop fusion | flops 11796480 | bytes 1449984 | tf_op jit(solution)/shard_map/concatenate | solution.py:253
  16.9 18.9 %collective-permute-done.1.down = bf16[538,4,256]{2,1,0:T(4,128)(2,1)S(1)} collective-permute-done((bf16[538,4,256]{2,1,0:T(4,128)(2,1)}, bf16[538,4,256]{2,1,0:T(4,128)(2,1)S(1)}, u32[]{:S(2)}, u32[]{:S(2)}) %collective-permute-start.1) | collective-permute-done | bytes 1101856 | tf_op jit(solution)/shard_map/ppermute | solution.py:260
  35.7 1.1 copy-done.1
  36.8 0.4 copy-done
  37.2 6.4 %first.1 = (bf16[4,256,256]{2,1,0:T(8,128)(2,1)}, bf16[4,1024,256]{2,1,0:T(8,128)(2,1)}, bf16[4,1024,256]{2,1,0:T(8,128)(2,1)}) custom-call(bf16[256,2304]{1,0:T(8,128)(2,1)} %fusion.7.slant, bf16[600,4,256]{2,1,0:T(4,128)(2,1)} %copy-done, bf16[538,4,256]{2,1,0:T(4,128)(2,1)} %copy-done.1, bf16[4,1024,256]{2,1,0:T(8,128)(2,1)} %get-tuple-element.18.mid), custom_call_target="tpu_custom_call" | custom-call | flops 1207959552 | bytes 10485760 | tf_op jit(solution)/shard_map/first/pallas_call | solution.py:148
  43.6 7.9 %rest.1 = (bf16[4,256,256]{2,1,0:T(8,128)(2,1)}, bf16[4,256,256]{2,1,0:T(8,128)(2,1)}, bf16[4,256,256]{2,1,0:T(8,128)(2,1)}) custom-call(bf16[256,2304]{1,0:T(8,128)(2,1)} %fusion.7.slant, bf16[4,1024,256]{2,1,0:T(8,128)(2,1)} %get-tuple-element.19.low, bf16[4,1024,256]{2,1,0:T(8,128)(2,1)} %get-tuple-element.18.mid, ...), custom_call_target="tpu_custom_call" | custom-call | flops 3623878656 | bytes 9437184 | tf_op jit(solution)/shard_map/rest/pallas_call | solution.py:172
  51.4 3.7 %collective-permute-start.7 = (bf16[4,256,256]{2,1,0:T(8,128)(2,1)}, bf16[4,256,256]{2,1,0:T(8,128)(2,1)S(1)}, u32[]{:S(2)}, u32[]{:S(2)}) collective-permute-start(bf16[4,256,256]{2,1,0:T(8,128)(2,1)} %get-tuple-element.23.own), channel_id=1, source_target_pairs={{1,0},{2,1},{3,2},{4,3},{5,4},{6,5},{7,6},{8,7},{9,8},{10,9},{11,1... | collective-permute-start | bytes 1572872 | tf_op jit(solution)/shard_map/ppermute | solution.py:260
  55.2 2.7 %collective-permute-start.9 = (bf16[4,256,256]{2,1,0:T(8,128)(2,1)S(1)}, bf16[4,256,256]{2,1,0:T(8,128)(2,1)S(1)}, u32[]{:S(2)}, u32[]{:S(2)}) collective-permute-start(bf16[4,256,256]{2,1,0:T(8,128)(2,1)S(1)} %copy-done.9), channel_id=1, source_target_pairs={{1,0},{2,1},{3,2},{4,3},{5,4},{6,5},{7,6},{8,7},{9,8},{10,9},{11,1... | collective-permute-start | bytes 1572872 | tf_op jit(solution)/shard_map/ppermute | solution.py:260
  57.8 4.4 %collective-permute-start.8 = (bf16[4,256,256]{2,1,0:T(8,128)(2,1)S(1)}, bf16[4,256,256]{2,1,0:T(8,128)(2,1)S(1)}, u32[]{:S(2)}, u32[]{:S(2)}) collective-permute-start(bf16[4,256,256]{2,1,0:T(8,128)(2,1)S(1)} %copy-done.9), channel_id=1, source_target_pairs={{0,1},{1,2},{2,3},{3,4},{4,5},{5,6},{6,7},{7,8},{8,9},{9,10},{10,1... | collective-permute-start | bytes 1572872 | tf_op jit(solution)/shard_map/ppermute | solution.py:260
  62.3 1.9 %collective-permute-start.6 = (bf16[4,256,256]{2,1,0:T(8,128)(2,1)}, bf16[4,256,256]{2,1,0:T(8,128)(2,1)S(1)}, u32[]{:S(2)}, u32[]{:S(2)}) collective-permute-start(bf16[4,256,256]{2,1,0:T(8,128)(2,1)} %get-tuple-element.23.own), channel_id=1, source_target_pairs={{0,1},{1,2},{2,3},{3,4},{4,5},{5,6},{6,7},{7,8},{8,9},{9,10},{10,1... | collective-permute-start | bytes 1572872 | tf_op jit(solution)/shard_map/ppermute | solution.py:260
  64.2 2.4 %collective-permute-start.5 = (bf16[4,256,256]{2,1,0:T(8,128)(2,1)}, bf16[4,256,256]{2,1,0:T(8,128)(2,1)S(1)}, u32[]{:S(2)}, u32[]{:S(2)}) collective-permute-start(bf16[4,256,256]{2,1,0:T(8,128)(2,1)} %get-tuple-element.22.own), channel_id=1, source_target_pairs={{1,0},{2,1},{3,2},{4,3},{5,4},{6,5},{7,6},{8,7},{9,8},{10,9},{11,1... | collective-permute-start | bytes 1572872 | tf_op jit(solution)/shard_map/ppermute | solution.py:260
  66.6 5.3 %collective-permute-start.4 = (bf16[4,256,256]{2,1,0:T(8,128)(2,1)}, bf16[4,256,256]{2,1,0:T(8,128)(2,1)S(1)}, u32[]{:S(2)}, u32[]{:S(2)}) collective-permute-start(bf16[4,256,256]{2,1,0:T(8,128)(2,1)} %get-tuple-element.22.own), channel_id=1, source_target_pairs={{0,1},{1,2},{2,3},{3,4},{4,5},{5,6},{6,7},{7,8},{8,9},{9,10},{10,1... | collective-permute-start | bytes 1572872 | tf_op jit(solution)/shard_map/ppermute | solution.py:260
  72.0 20.9 %collective-permute-done.9.following = bf16[4,256,256]{2,1,0:T(8,128)(2,1)S(1)} collective-permute-done((bf16[4,256,256]{2,1,0:T(8,128)(2,1)S(1)}, bf16[4,256,256]{2,1,0:T(8,128)(2,1)S(1)}, u32[]{:S(2)}, u32[]{:S(2)}) %collective-permute-start.9) | collective-permute-done | bytes 524320 | tf_op jit(solution)/shard_map/ppermute | solution.py:260
  92.8 0.8 copy-done.10
  93.7 1.9 %collective-permute-start.3 = (bf16[4,256,256]{2,1,0:T(8,128)(2,1)}, bf16[4,256,256]{2,1,0:T(8,128)(2,1)S(1)}, u32[]{:S(2)}, u32[]{:S(2)}) collective-permute-start(bf16[4,256,256]{2,1,0:T(8,128)(2,1)} %get-tuple-element.21.own), channel_id=1, source_target_pairs={{1,0},{2,1},{3,2},{4,3},{5,4},{6,5},{7,6},{8,7},{9,8},{10,9},{11,1... | collective-permute-start | bytes 1572872 | tf_op jit(solution)/shard_map/ppermute | solution.py:260
  95.6 0.8 copy-done.11
  96.4 5.3 %collective-permute-start.2 = (bf16[4,256,256]{2,1,0:T(8,128)(2,1)}, bf16[4,256,256]{2,1,0:T(8,128)(2,1)S(1)}, u32[]{:S(2)}, u32[]{:S(2)}) collective-permute-start(bf16[4,256,256]{2,1,0:T(8,128)(2,1)} %get-tuple-element.21.own), channel_id=1, source_target_pairs={{0,1},{1,2},{2,3},{3,4},{4,5},{5,6},{6,7},{7,8},{8,9},{9,10},{10,1... | collective-permute-start | bytes 1572872 | tf_op jit(solution)/shard_map/ppermute | solution.py:260
  101.7 5.3 %smooth.4.rest_0_ = bf16[64,16,4,256]{3,2,1,0:T(4,128)(2,1)} custom-call(f32[27,64,256]{2,1,0:T(8,128)} %get-tuple-element.15.weights, bf16[4,256,256]{2,1,0:T(8,128)(2,1)} %copy-done.11, bf16[4,256,256]{2,1,0:T(8,128)(2,1)} %get-tuple-element.24.own, bf16[4,256,256]{2,1,0:T(8,128)(2,1)} %copy-done.10), custom_call_target="tpu_custom_call" | custom-call | flops 14155776 | bytes 3145728 | tf_op jit(solution)/shard_map/smooth/pallas_call | solution.py:227
  107.0 0.8 copy-done.6
  107.8 5.3 %smooth.5.rest_0_ = bf16[64,16,4,256]{3,2,1,0:T(4,128)(2,1)} custom-call(f32[27,64,256]{2,1,0:T(8,128)} %get-tuple-element.15.weights, bf16[4,256,256]{2,1,0:T(8,128)(2,1)} %copy-done.6, bf16[4,256,256]{2,1,0:T(8,128)(2,1)} %get-tuple-element.23.own, bf16[4,256,256]{2,1,0:T(8,128)(2,1)} %copy-done.3, ...), custom_call_target="tpu_custom_call", output_to_operand_aliasing={{}: (4, {})} | custom-call | flops 14155776 | bytes 3145728 | tf_op jit(solution)/shard_map/smooth/pallas_call | solution.py:227
  113.1 0.8 copy-done.4
  113.9 0.8 copy-done.7
  114.7 5.3 %smooth.6.rest_0_ = bf16[64,16,4,256]{3,2,1,0:T(4,128)(2,1)} custom-call(f32[27,64,256]{2,1,0:T(8,128)} %get-tuple-element.15.weights, bf16[4,256,256]{2,1,0:T(8,128)(2,1)} %copy-done.7, bf16[4,256,256]{2,1,0:T(8,128)(2,1)} %get-tuple-element.22.own, bf16[4,256,256]{2,1,0:T(8,128)(2,1)} %copy-done.4, ...), custom_call_target="tpu_custom_call", output_to_operand_aliasing={{}: (4, {})} | custom-call | flops 14155776 | bytes 3145728 | tf_op jit(solution)/shard_map/smooth/pallas_call | solution.py:227
  120.0 0.8 copy-done.5
  120.8 0.8 copy-done.8
  121.6 5.3 %smooth.7 = bf16[64,16,4,256]{3,2,1,0:T(4,128)(2,1)} custom-call(f32[27,64,256]{2,1,0:T(8,128)} %get-tuple-element.15.weights, bf16[4,256,256]{2,1,0:T(8,128)(2,1)} %copy-done.8, bf16[4,256,256]{2,1,0:T(8,128)(2,1)} %get-tuple-element.21.own, bf16[4,256,256]{2,1,0:T(8,128)(2,1)} %copy-done.5, ...), custom_call_target="tpu_custom_call", output_to_operand_aliasing={{}: (4, {})} | custom-call | flops 14155776 | bytes 3145728 | tf_op jit(solution)/shard_map/smooth/pallas_call | solution.py:227
  (31 shorter events, 0.8 us)
Async XLA Ops:
  0.0 8.8 %copy-start.12 = (s32[16,4,256]{2,1,0:T(4,128)S(1)}, s32[16,4,256]{2,1,0:T(4,128)}, u32[]{:S(2)}) copy-start(s32[16,4,256]{2,1,0:T(4,128)} %param.6) | copy-start | bytes 196612
  0.0 9.4 %copy-start.13 = (s32[64]{0:T(128)S(1)}, s32[64]{0:T(128)}, u32[]{:S(2)}) copy-start(s32[64]{0:T(128)} %param.8) | copy-start | bytes 772
  0.0 9.5 %copy-start.2 = (bf16[64,64,33]{1,0,2:T(8,128)(2,1)S(1)}, bf16[64,64,33]{1,0,2:T(8,128)(2,1)}, u32[]{:S(2)}) copy-start(bf16[64,64,33]{1,0,2:T(8,128)(2,1)} %param.7) | copy-start | bytes 811012
  3.5 32.2 %collective-permute-start = (bf16[600,4,256]{2,1,0:T(4,128)(2,1)}, bf16[600,4,256]{2,1,0:T(4,128)(2,1)S(1)}, u32[]{:S(2)}, u32[]{:S(2)}) collective-permute-start(bf16[600,4,256]{2,1,0:T(4,128)(2,1)} %get-tuple-element.16), channel_id=1, source_target_pairs={{0,32},{32,64},{64,96},{96,128},{128,160},{160,192},{192,224},{1,3... | collective-permute-start | bytes 3686408 | tf_op jit(solution)/shard_map/ppermute | solution.py:260
  6.6 29.1 %collective-permute-start.1 = (bf16[538,4,256]{2,1,0:T(4,128)(2,1)}, bf16[538,4,256]{2,1,0:T(4,128)(2,1)S(1)}, u32[]{:S(2)}, u32[]{:S(2)}) collective-permute-start(bf16[538,4,256]{2,1,0:T(4,128)(2,1)} %get-tuple-element.17), channel_id=1, source_target_pairs={{32,0},{64,32},{96,64},{128,96},{160,128},{192,160},{224,192},{33,... | collective-permute-start | bytes 3305480 | tf_op jit(solution)/shard_map/ppermute | solution.py:260
  35.7 1.1 copy-start.1
  35.7 1.4 %copy-start = (bf16[600,4,256]{2,1,0:T(4,128)(2,1)}, bf16[600,4,256]{2,1,0:T(4,128)(2,1)S(1)}, u32[]{:S(2)}) copy-start(bf16[600,4,256]{2,1,0:T(4,128)(2,1)S(1)} %collective-permute-done.up) | copy-start | bytes 3686404
  43.6 11.6 %copy-start.9 = (bf16[4,256,256]{2,1,0:T(8,128)(2,1)S(1)}, bf16[4,256,256]{2,1,0:T(8,128)(2,1)}, u32[]{:S(2)}) copy-start(bf16[4,256,256]{2,1,0:T(8,128)(2,1)} %get-tuple-element.24.own) | copy-start | bytes 1572868
  51.4 15.2 %collective-permute-start.7 = (bf16[4,256,256]{2,1,0:T(8,128)(2,1)}, bf16[4,256,256]{2,1,0:T(8,128)(2,1)S(1)}, u32[]{:S(2)}, u32[]{:S(2)}) collective-permute-start(bf16[4,256,256]{2,1,0:T(8,128)(2,1)} %get-tuple-element.23.own), channel_id=1, source_target_pairs={{1,0},{2,1},{3,2},{4,3},{5,4},{6,5},{7,6},{8,7},{9,8},{10,9},{11,1... | collective-permute-start | bytes 1572872 | tf_op jit(solution)/shard_map/ppermute | solution.py:260
  55.2 37.6 %collective-permute-start.9 = (bf16[4,256,256]{2,1,0:T(8,128)(2,1)S(1)}, bf16[4,256,256]{2,1,0:T(8,128)(2,1)S(1)}, u32[]{:S(2)}, u32[]{:S(2)}) collective-permute-start(bf16[4,256,256]{2,1,0:T(8,128)(2,1)S(1)} %copy-done.9), channel_id=1, source_target_pairs={{1,0},{2,1},{3,2},{4,3},{5,4},{6,5},{7,6},{8,7},{9,8},{10,9},{11,1... | collective-permute-start | bytes 1572872 | tf_op jit(solution)/shard_map/ppermute | solution.py:260
  57.8 37.7 %collective-permute-start.8 = (bf16[4,256,256]{2,1,0:T(8,128)(2,1)S(1)}, bf16[4,256,256]{2,1,0:T(8,128)(2,1)S(1)}, u32[]{:S(2)}, u32[]{:S(2)}) collective-permute-start(bf16[4,256,256]{2,1,0:T(8,128)(2,1)S(1)} %copy-done.9), channel_id=1, source_target_pairs={{0,1},{1,2},{2,3},{3,4},{4,5},{5,6},{6,7},{7,8},{8,9},{9,10},{10,1... | collective-permute-start | bytes 1572872 | tf_op jit(solution)/shard_map/ppermute | solution.py:260
  62.3 44.7 %collective-permute-start.6 = (bf16[4,256,256]{2,1,0:T(8,128)(2,1)}, bf16[4,256,256]{2,1,0:T(8,128)(2,1)S(1)}, u32[]{:S(2)}, u32[]{:S(2)}) collective-permute-start(bf16[4,256,256]{2,1,0:T(8,128)(2,1)} %get-tuple-element.23.own), channel_id=1, source_target_pairs={{0,1},{1,2},{2,3},{3,4},{4,5},{5,6},{6,7},{7,8},{8,9},{9,10},{10,1... | collective-permute-start | bytes 1572872 | tf_op jit(solution)/shard_map/ppermute | solution.py:260
  64.2 48.9 %collective-permute-start.5 = (bf16[4,256,256]{2,1,0:T(8,128)(2,1)}, bf16[4,256,256]{2,1,0:T(8,128)(2,1)S(1)}, u32[]{:S(2)}, u32[]{:S(2)}) collective-permute-start(bf16[4,256,256]{2,1,0:T(8,128)(2,1)} %get-tuple-element.22.own), channel_id=1, source_target_pairs={{1,0},{2,1},{3,2},{4,3},{5,4},{6,5},{7,6},{8,7},{9,8},{10,9},{11,1... | collective-permute-start | bytes 1572872 | tf_op jit(solution)/shard_map/ppermute | solution.py:260
  66.6 40.4 %copy-start.3 = (bf16[4,256,256]{2,1,0:T(8,128)(2,1)}, bf16[4,256,256]{2,1,0:T(8,128)(2,1)S(1)}, u32[]{:S(2)}) copy-start(bf16[4,256,256]{2,1,0:T(8,128)(2,1)S(1)} %collective-permute-done.7.following) | copy-start | bytes 1572868
  66.6 46.5 %collective-permute-start.4 = (bf16[4,256,256]{2,1,0:T(8,128)(2,1)}, bf16[4,256,256]{2,1,0:T(8,128)(2,1)S(1)}, u32[]{:S(2)}, u32[]{:S(2)}) collective-permute-start(bf16[4,256,256]{2,1,0:T(8,128)(2,1)} %get-tuple-element.22.own), channel_id=1, source_target_pairs={{0,1},{1,2},{2,3},{3,4},{4,5},{5,6},{6,7},{7,8},{8,9},{9,10},{10,1... | collective-permute-start | bytes 1572872 | tf_op jit(solution)/shard_map/ppermute | solution.py:260
  92.8 0.8 copy-start.10
  93.7 26.4 %collective-permute-start.3 = (bf16[4,256,256]{2,1,0:T(8,128)(2,1)}, bf16[4,256,256]{2,1,0:T(8,128)(2,1)S(1)}, u32[]{:S(2)}, u32[]{:S(2)}) collective-permute-start(bf16[4,256,256]{2,1,0:T(8,128)(2,1)} %get-tuple-element.21.own), channel_id=1, source_target_pairs={{1,0},{2,1},{3,2},{4,3},{5,4},{6,5},{7,6},{8,7},{9,8},{10,9},{11,1... | collective-permute-start | bytes 1572872 | tf_op jit(solution)/shard_map/ppermute | solution.py:260
  95.6 0.8 copy-start.11
  96.4 23.7 %collective-permute-start.2 = (bf16[4,256,256]{2,1,0:T(8,128)(2,1)}, bf16[4,256,256]{2,1,0:T(8,128)(2,1)S(1)}, u32[]{:S(2)}, u32[]{:S(2)}) collective-permute-start(bf16[4,256,256]{2,1,0:T(8,128)(2,1)} %get-tuple-element.21.own), channel_id=1, source_target_pairs={{0,1},{1,2},{2,3},{3,4},{4,5},{5,6},{6,7},{7,8},{8,9},{9,10},{10,1... | collective-permute-start | bytes 1572872 | tf_op jit(solution)/shard_map/ppermute | solution.py:260
  107.0 0.8 copy-start.6
  113.1 0.8 copy-start.4
  113.9 0.8 copy-start.7
  120.0 0.8 copy-start.5
  120.8 0.8 copy-start.8
